TPU v7x, 32 devices: a whole 2x2x4 slice. The times are simulated.
32 devices in a mesh: groups: 2 (over x), row: 16 (over z, y, core).
Axes of the slice: x: 2, y: 2, z: 4, core: 2. Of those that a mesh axis runs over, the one named last changes fastest.
Arguments:
- bound_coeff: bfloat16 [4, 64, 8192], P('groups', 'row'), parts along dimension 0, may hold values from -0.044 to 0.044
- status: int32 [4, 8192], P('groups'), parts along dimension 0, may hold values from 0 to 2
- slope_bit: int32 [4, 8192], P('groups'), parts along dimension 0, may hold values from 0 to 1
- pre_lower: float32 [4, 8192], P('groups'), parts along dimension 0, may hold values from -2 to -0.1
- pre_upper: float32 [4, 8192], P('groups'), parts along dimension 0, may hold values from 0.1 to 2
- weight: bfloat16 [16384, 8192], P('groups', 'row'), parts along dimension 0, may hold values from -0.0625 to 0.0625
- layer_bias: float32 [16384], P('groups'), parts along dimension 0, may hold values from -6 to 6
- center_input: float32 [4, 8192], P('groups', 'row'), parts along dimension 0, may hold values from -6 to 6
- radius: float32 [4, 8192], P('groups', 'row'), parts along dimension 0, may hold values from 0.05 to 1
Outputs:
- lower_bound: float32 [4, 64], P('groups', 'row'), parts along dimension 0
- upper_bound: float32 [4, 64], P('groups', 'row'), parts along dimension 0
There are 2 independent parts, one for each index of `groups`. A program takes and returns all parts, laid end to end along the dimension named above; each array names one. Nothing has to cross between parts.
All inputs are finite; a program needn't handle non-finite values.
Results may differ from a plain program's by a relative error of at most 0.0003.
Values may be sent and summed in bfloat16 or wider, within the bound.
No kernel may reach another device: no remote copies, remote signals or barrier semaphores. Data moves between devices by JAX's collectives and lax.ppermute only.
A program may use at most 64 MiB of HBM per device.

v0:
```python
import jax
import jax.numpy as jnp
from jax import lax
from jax.sharding import PartitionSpec as P


def relax_coeff(bound_coeff, status, slope_bit, pre_lower, pre_upper):
    values = bound_coeff.astype(jnp.float32)
    upper_slope = (pre_upper / (pre_upper - pre_lower))[:, None, :]
    chosen = slope_bit.astype(jnp.float32)[:, None, :]
    unstable = (status == 2)[:, None, :]
    active = (status == 1)[:, None, :]
    positive = values >= 0.0
    slope_low = jnp.where(
        active, 1.0, jnp.where(unstable, jnp.where(positive, chosen, upper_slope), 0.0)
    )
    slope_up = jnp.where(
        active, 1.0, jnp.where(unstable, jnp.where(positive, upper_slope, chosen), 0.0)
    )
    return ((values * slope_low).astype(jnp.bfloat16), (values * slope_up).astype(jnp.bfloat16))


def intercepts(bound_coeff, status, pre_lower, pre_upper):
    values = bound_coeff.astype(jnp.float32)
    upper_slope = pre_upper / (pre_upper - pre_lower)
    offset = (-upper_slope * pre_lower)[:, None, :]
    unstable = (status == 2)[:, None, :]
    positive = values >= 0.0
    below_term = jnp.sum(
        jnp.where(unstable & jnp.logical_not(positive), values * offset, 0.0), axis=-1
    )
    above_term = jnp.sum(jnp.where(unstable & positive, values * offset, 0.0), axis=-1)
    return (below_term, above_term)


def on_device(
    bound_coeff, status, slope_bit, pre_lower, pre_upper, weight, layer_bias, center_input, radius
):
    examples = bound_coeff.shape[0]
    num_neurons = bound_coeff.shape[2]
    local_cols = weight.shape[1]
    sign_pair = jnp.array([-1.0, 1.0], dtype=jnp.float32)
    part_center = jnp.einsum(
        "jd,ed->ej", weight.astype(jnp.float32), center_input, precision=lax.Precision.HIGHEST
    )
    center = lax.psum(part_center, "row") + layer_bias[None, :]
    relaxed_low, relaxed_up = relax_coeff(bound_coeff, status, slope_bit, pre_lower, pre_upper)
    below_term, above_term = intercepts(bound_coeff, status, pre_lower, pre_upper)
    stacked = lax.all_gather(jnp.stack([relaxed_low, relaxed_up]), "row", axis=2, tiled=True)
    num_rows = stacked.shape[2]
    flat_rows = stacked.reshape(2 * examples * num_rows, num_neurons)
    mapped = jnp.dot(flat_rows, weight, preferred_element_type=jnp.float32).reshape(
        2, examples, num_rows, local_cols
    )
    result = sign_pair[:, None, None] * jnp.einsum(
        "lerd,ed->ler", jnp.abs(mapped), radius, precision=lax.Precision.HIGHEST
    )
    summed = lax.psum_scatter(result, "row", scatter_dimension=2, tiled=True)
    near_low = jnp.einsum(
        "erj,ej->er", relaxed_low.astype(jnp.float32), center, precision=lax.Precision.HIGHEST
    )
    near_up = jnp.einsum(
        "erj,ej->er", relaxed_up.astype(jnp.float32), center, precision=lax.Precision.HIGHEST
    )
    lower_bound = near_low + below_term + summed[0]
    upper_bound = near_up + above_term + summed[1]
    return (lower_bound, upper_bound)


def solution(mesh):
    in_specs = (
        P("groups", "row", None),
        P("groups", None),
        P("groups", None),
        P("groups", None),
        P("groups", None),
        P("groups", "row"),
        P("groups"),
        P("groups", "row"),
        P("groups", "row"),
    )
    out_specs = (P("groups", "row"), P("groups", "row"))
    return jax.shard_map(
        on_device, mesh=mesh, in_specs=in_specs, out_specs=out_specs, check_vma=False
    )
```

profile of v0, /device:TPU:0, one launch (start us, length us, event | category | flops | bytes accessed | tf_op | source)
XLA Modules:
  0.0 207.5 jit_solution(9305162727291835596)
XLA Ops:
  7.3 0.6 copy-done
  7.9 9.5 %fusion.24 = f32[2,8192]{1,0:T(2,128)} fusion(f32[2,512]{1,0:T(2,128)S(1)} %copy-done, bf16[8192,512]{1,0:T(8,128)(2,1)} %param.15), kind=kOutput, calls=%fused_computation.37 | convolution fusion | flops 100663296 | bytes 8458240 | tf_op jit(solution)/shard_map/jd,ed->ej/dot_general | solution.py:43
  17.4 0.0 all-gather.2.cloned.1.call-start
  17.5 0.1 broadcast_compare_fusion.1
  17.6 0.1 negate_multiply_fusion
  17.7 1.1 fusion.12
  18.8 1.0 pad_maximum_fusion
  19.8 0.6 dynamic-slice
  21.1 83.7 %all-reduce.3.cloned.1.call-done = f32[2,8192]{1,0:T(2,128)} async-done(((f32[2,8192]{1,0:T(2,128)}), f32[2,8192]{1,0:T(2,128)}) %all-reduce.3.cloned.1.call-update) | async-done | bytes 65552 | tf_op jit(solution)/shard_map/psum | solution.py:46
  104.7 0.9 add_bitcast_fusion
  105.6 0.7 fusion.16
  106.3 0.1 copy.23
  106.4 0.7 fusion.14
  107.2 0.1 copy.29
  107.3 52.0 %all-gather.2.cloned.1.call-done = bf16[2,2,64,8192]{3,1,0,2:T(2,128)(2,1)} async-done(((bf16[2,2,4,8192]{3,1,0,2:T(2,128)(2,1)}), bf16[2,2,64,8192]{3,1,0,2:T(2,128)(2,1)}) %all-gather.2.cloned.1.call-update) | async-done | bytes 4194320 | tf_op jit(solution)/shard_map/all_gather | solution.py:49
  159.3 7.8 %fusion.3 = f32[2,2,64,512]{3,2,1,0:T(8,128)S(1)} fusion(bf16[8192,512]{1,0:T(8,128)(2,1)} %param.15, bf16[2,2,64,8192]{3,1,0,2:T(2,128)(2,1)} %all-gather.2.cloned.1.call-done), kind=kOutput, calls=%fused_computation.3 | convolution fusion | flops 2147614720 | bytes 13107200 | tf_op jit(solution)/shard_map/dot_general | solution.py:52
  167.1 0.7 fusion.8
  167.8 0.1 fusion.22
  167.9 31.1 %all-reduce = f32[2,2,64]{2,1,0:T(2,128)S(1)} all-reduce(f32[2,2,64]{2,1,0:T(2,128)S(1)} %fusion.22), channel_id=2, replica_groups=mesh['groups'=2,'row'=16] {'row'}, use_global_device_ids=true, to_apply=%region_2.3.clone | all-reduce | flops 256 | bytes 2048
  199.1 0.1 dynamic-slice_bitcast_fusion
  199.1 0.1 copy.18
  199.2 0.1 copy.17
  199.3 0.7 copy.20
  200.0 0.6 copy.19
  (24 shorter events, 0.1 us)
Async XLA Ops:
  7.2 0.7 copy-start
  7.2 12.7 %copy-start.9 = (u32[32]{0:T(128)S(1)}, u32[32]{0:T(128)}, u32[]{:S(2)}) copy-start(u32[32]{0:T(128)} %constant.15) | copy-start | bytes 388
  7.2 10.3 %copy-start.2 = (s32[2,8192]{1,0:T(2,128)S(1)}, s32[2,8192]{1,0:T(2,128)}, u32[]{:S(2)}) copy-start(s32[2,8192]{1,0:T(2,128)} %param.12) | copy-start | bytes 196612
  7.2 10.3 %copy-start.3 = (s32[2,8192]{1,0:T(2,128)S(1)}, s32[2,8192]{1,0:T(2,128)}, u32[]{:S(2)}) copy-start(s32[2,8192]{1,0:T(2,128)} %param.11) | copy-start | bytes 196612
  7.2 10.4 %copy-start.5 = (f32[2,8192]{1,0:T(2,128)S(1)}, f32[2,8192]{1,0:T(2,128)}, u32[]{:S(2)}) copy-start(f32[2,8192]{1,0:T(2,128)} %param.14) | copy-start | bytes 196612
  7.2 10.4 %copy-start.4 = (f32[2,8192]{1,0:T(2,128)S(1)}, f32[2,8192]{1,0:T(2,128)}, u32[]{:S(2)}) copy-start(f32[2,8192]{1,0:T(2,128)} %param.13) | copy-start | bytes 196612
  7.2 10.5 %copy-start.1 = (bf16[2,4,8192]{2,1,0:T(4,128)(2,1)S(1)}, bf16[2,4,8192]{2,1,0:T(4,128)(2,1)}, u32[]{:S(2)}) copy-start(bf16[2,4,8192]{2,1,0:T(4,128)(2,1)} %param.10) | copy-start | bytes 393220
  7.2 97.5 %copy-start.6 = (f32[8192]{0:T(1024)S(1)}, f32[8192]{0:T(1024)}, u32[]{:S(2)}) copy-start(f32[8192]{0:T(1024)} %param.16) | copy-start | bytes 98308
  7.3 97.5 %all-reduce.3.cloned.1.call-start = ((), (), s32[]{:S(2)}) async-start(), calls=%async_computation | async-start | bytes 131072 | tf_op jit(solution)/shard_map/psum | solution.py:46
  17.4 141.9 %all-gather.2.cloned.1.call-start = ((), (), s32[]{:S(2)}) async-start(), calls=%async_computation.1 | async-start | bytes 4456448 | tf_op jit(solution)/shard_map/all_gather | solution.py:49
  107.3 59.8 %copy-start.7 = (f32[2,512]{1,0:T(2,128)S(1)}, f32[2,512]{1,0:T(2,128)}, u32[]{:S(2)}) copy-start(f32[2,512]{1,0:T(2,128)} %param.18) | copy-start | bytes 12292
  107.3 60.5 %copy-start.8 = (f32[2]{0:T(128)S(1)}, f32[2]{0:T(128)}, u32[]{:S(2)}) copy-start(f32[2]{0:T(128)} %constant.4.clone) | copy-start | bytes 28
Sparse Core Ops, SparseCore 0:
  17.5 87.1 all-reduce.2
  107.1 52.1 all-gather.1
where the time goes:
time: 208 us; the launch traced here: 207 us
  waiting for transfers between devices  136 us (65%)
  blocking collectives  31.1 us (15%)
  matrix products  19.5 us (9%)
  between operations  14.9 us (7%)
  other arithmetic  3.24 us (2%)
  local copies, waits for them, and re-layouts  2.94 us (1%)
    psum x1, waiting for transfers between devices, on_device(): center = lax.psum(part_center, 'row') + layer_bias[None, :]  83.7 us
    all_gather x1, waiting for transfers between devices, on_device(): lax.all_gather(jnp.stack([relaxed_low, relaxed_up]), 'row', axis=2, tiled...  52 us
    unnamed x1, blocking collectives  31.1 us
    dot_general x1, matrix products, on_device(): jnp.einsum('jd,ed->ej', weight.astype(jnp.float32), center_input, precisi...  9.53 us
    dot_general x1, matrix products, on_device(): jnp.dot(flat_rows, weight, preferred_element_type=jnp.float32)  7.77 us
  transfers between devices with their start and end apart: 2, of which 2 were waited for; matrix products, arithmetic and copies ran while one was open for 3% of the time, Pallas kernels for 0%

commit v1 on v0

--- a/solution.py
+++ b/solution.py
@@ -43,7 +43,7 @@
     part_center = jnp.einsum(
         "jd,ed->ej", weight.astype(jnp.float32), center_input, precision=lax.Precision.HIGHEST
     )
-    center = lax.psum(part_center, "row") + layer_bias[None, :]
+    center = jnp.sum(lax.all_gather(part_center, "row"), axis=0) + layer_bias[None, :]
     relaxed_low, relaxed_up = relax_coeff(bound_coeff, status, slope_bit, pre_lower, pre_upper)
     below_term, above_term = intercepts(bound_coeff, status, pre_lower, pre_upper)
     stacked = lax.all_gather(jnp.stack([relaxed_low, relaxed_up]), "row", axis=2, tiled=True)

time: 208 us -> 158 us (0.76)
  waiting for transfers between devices: 136 us -> 85.5 us
    psum x1 -> x0, waiting for transfers between devices: 83.7 us -> none  [on_device(): center = lax.psum(part_center, 'row') + layer_bias[None, :]]
    all_gather x0 -> x1, waiting for transfers between devices: none -> 37.1 us  [on_device(): lax.all_gather(part_center, 'row')]
    all_gather x1, waiting for transfers between devices: 52 us -> 48.4 us  [on_device(): lax.all_gather(jnp.stack([relaxed_low, relaxed_up]), 'row', axis=2, tiled...]
  transfers between devices with their start and end apart: 2 -> 2, of which waited for: 2 -> 2; matrix products, arithmetic and copies ran while one was open for 3% -> 4% of each run, Pallas kernels for 0% -> 0%
where the time goes in v1:
time: 158 us
  waiting for transfers between devices  85.5 us (54%)
  blocking collectives  31.1 us (20%)
  matrix products  19.5 us (12%)
  between operations  14.9 us (9%)
  other arithmetic  3.99 us (3%)
  local copies, waits for them, and re-layouts  2.94 us (2%)
    all_gather x1, waiting for transfers between devices, on_device(): lax.all_gather(jnp.stack([relaxed_low, relaxed_up]), 'row', axis=2, tiled...  48.4 us
    all_gather x1, waiting for transfers between devices, on_device(): lax.all_gather(part_center, 'row')  37.1 us
    unnamed x1, blocking collectives  31.1 us
    dot_general x1, matrix products, on_device(): jnp.einsum('jd,ed->ej', weight.astype(jnp.float32), center_input, precisi...  9.53 us
    dot_general x1, matrix products, on_device(): jnp.dot(flat_rows, weight, preferred_element_type=jnp.float32)  7.78 us
  transfers between devices with their start and end apart: 2, of which 2 were waited for; matrix products, arithmetic and copies ran while one was open for 4% of the time, Pallas kernels for 0%

profile of v1, /device:TPU:0, one launch (start us, length us, event | category | flops | bytes accessed | tf_op | source)
XLA Modules:
  0.0 158.0 jit_solution(9611789087720370596)
XLA Ops:
  7.3 0.6 copy-done
  7.9 9.5 %convolution_bitcast_fusion = f32[1,2,8192]{2,1,0:T(2,128)} fusion(f32[2,512]{1,0:T(2,128)S(1)} %copy-done, bf16[8192,512]{1,0:T(8,128)(2,1)} %param.15), kind=kOutput, calls=%fused_computation | convolution fusion | flops 100663296 | bytes 8458240 | tf_op jit(solution)/shard_map/jd,ed->ej/dot_general | solution.py:43
  17.4 0.0 all-gather.5.cloned.1.call-start
  17.5 0.1 negate_multiply_fusion
  17.6 0.1 broadcast_compare_fusion.1
  17.7 1.1 fusion.12
  18.8 1.1 pad_maximum_fusion
  19.9 0.6 dynamic-slice
  21.1 37.1 %all-gather.7.cloned.1.call-done = f32[16,2,8192]{2,1,0:T(2,128)} async-done(((f32[1,2,8192]{2,1,0:T(2,128)}), f32[16,2,8192]{2,1,0:T(2,128)}) %all-gather.7.cloned.1.call-update) | async-done | bytes 1048592 | tf_op jit(solution)/shard_map/all_gather | solution.py:46
  58.2 1.6 reduce_sum.27
  59.8 0.7 fusion.16
  60.6 0.1 copy.23
  60.6 0.7 fusion.14
  61.4 0.1 copy.29
  61.5 48.4 %all-gather.5.cloned.1.call-done = bf16[2,2,64,8192]{3,1,0,2:T(2,128)(2,1)} async-done(((bf16[2,2,4,8192]{3,1,0,2:T(2,128)(2,1)}), bf16[2,2,64,8192]{3,1,0,2:T(2,128)(2,1)}) %all-gather.5.cloned.1.call-update) | async-done | bytes 4194320 | tf_op jit(solution)/shard_map/all_gather | solution.py:49
  109.9 7.8 %fusion.3 = f32[2,2,64,512]{3,2,1,0:T(8,128)S(1)} fusion(bf16[8192,512]{1,0:T(8,128)(2,1)} %param.15, bf16[2,2,64,8192]{3,1,0,2:T(2,128)(2,1)} %all-gather.5.cloned.1.call-done), kind=kOutput, calls=%fused_computation.4 | convolution fusion | flops 2147614720 | bytes 13107200 | tf_op jit(solution)/shard_map/dot_general | solution.py:52
  117.7 0.7 fusion.8
  118.4 0.1 fusion.22
  118.5 31.1 %all-reduce = f32[2,2,64]{2,1,0:T(2,128)S(1)} all-reduce(f32[2,2,64]{2,1,0:T(2,128)S(1)} %fusion.22), channel_id=3, replica_groups=mesh['groups'=2,'row'=16] {'row'}, use_global_device_ids=true, to_apply=%region_2.3.clone | all-reduce | flops 256 | bytes 2048
  149.6 0.1 dynamic-slice_bitcast_fusion
  149.7 0.1 copy.18
  149.8 0.1 copy.17
  149.9 0.7 copy.20
  150.5 0.6 copy.19
  (25 shorter events, 0.2 us)
Async XLA Ops:
  7.2 0.7 copy-start
  7.2 12.7 %copy-start.9 = (u32[32]{0:T(128)S(1)}, u32[32]{0:T(128)}, u32[]{:S(2)}) copy-start(u32[32]{0:T(128)} %constant.15) | copy-start | bytes 388
  7.2 10.3 %copy-start.5 = (f32[2,8192]{1,0:T(2,128)S(1)}, f32[2,8192]{1,0:T(2,128)}, u32[]{:S(2)}) copy-start(f32[2,8192]{1,0:T(2,128)} %param.14) | copy-start | bytes 196612
  7.2 10.3 %copy-start.4 = (f32[2,8192]{1,0:T(2,128)S(1)}, f32[2,8192]{1,0:T(2,128)}, u32[]{:S(2)}) copy-start(f32[2,8192]{1,0:T(2,128)} %param.13) | copy-start | bytes 196612
  7.2 10.3 %copy-start.2 = (s32[2,8192]{1,0:T(2,128)S(1)}, s32[2,8192]{1,0:T(2,128)}, u32[]{:S(2)}) copy-start(s32[2,8192]{1,0:T(2,128)} %param.11) | copy-start | bytes 196612
  7.2 10.4 %copy-start.3 = (s32[2,8192]{1,0:T(2,128)S(1)}, s32[2,8192]{1,0:T(2,128)}, u32[]{:S(2)}) copy-start(s32[2,8192]{1,0:T(2,128)} %param.12) | copy-start | bytes 196612
  7.2 10.5 %copy-start.1 = (bf16[2,4,8192]{2,1,0:T(4,128)(2,1)S(1)}, bf16[2,4,8192]{2,1,0:T(4,128)(2,1)}, u32[]{:S(2)}) copy-start(bf16[2,4,8192]{2,1,0:T(4,128)(2,1)} %param.10) | copy-start | bytes 393220
  7.2 52.5 %copy-start.6 = (f32[8192]{0:T(1024)S(1)}, f32[8192]{0:T(1024)}, u32[]{:S(2)}) copy-start(f32[8192]{0:T(1024)} %param.16) | copy-start | bytes 98308
  7.3 51.0 %all-gather.7.cloned.1.call-start = ((), (), s32[]{:S(2)}) async-start(), calls=%async_computation.1 | async-start | bytes 1114112 | tf_op jit(solution)/shard_map/all_gather | solution.py:46
  17.4 92.5 %all-gather.5.cloned.1.call-start = ((), (), s32[]{:S(2)}) async-start(), calls=%async_computation | async-start | bytes 4456448 | tf_op jit(solution)/shard_map/all_gather | solution.py:49
  61.5 56.2 %copy-start.7 = (f32[2,512]{1,0:T(2,128)S(1)}, f32[2,512]{1,0:T(2,128)}, u32[]{:S(2)}) copy-start(f32[2,512]{1,0:T(2,128)} %param.18) | copy-start | bytes 12292
  61.5 56.9 %copy-start.8 = (f32[2]{0:T(128)S(1)}, f32[2]{0:T(128)}, u32[]{:S(2)}) copy-start(f32[2]{0:T(128)} %constant.4.clone) | copy-start | bytes 28
Sparse Core Ops, SparseCore 0:
  17.5 40.6 all-gather.6
  60.4 49.4 all-gather.4
